TPU v7x, 128 devices: a whole 4x4x4 slice. The times are simulated.
128 devices in a mesh: wide: 16 (over y_lo, z, core), narrow: 8 (over x, y_hi).
Axes of the slice: x: 4, y: 4 (y_hi: 2, y_lo: 2; y = y_hi * 2 + y_lo), z: 4, core: 2. Of those that a mesh axis runs over, the one named last changes fastest.
Arguments:
- fields: float32 [5, 16, 64, 256], P(None, 'wide', 'narrow'), may hold values from -2.1 to 6.1, as said below
- prior_modes: bfloat16 [124, 5, 16, 16384], P(None, None, 'wide', 'narrow'), may hold values from -360 to 360, as said below
Outputs:
- flow_state: float32 [5, 16, 64, 256], P(None, 'wide', 'narrow')
- factor: float32 [128, 128], replicated
Inputs may be any that keep to these rules, and one draw needn't show every extreme that they name: `fields`: density and pressure lie in 0.6 to 1.4, each velocity component below 1.5 in magnitude. `prior_modes`: the columns are linearly independent.
All inputs are finite; a program needn't handle non-finite values.
Results may differ from a plain program's by a relative error of at most 0.0014.
Values may be sent and summed in bfloat16 or wider, within the bound.
No kernel may reach another device: no remote copies, remote signals or barrier semaphores. Data moves between devices by JAX's collectives and lax.ppermute only.
A program may use at most 64 MiB of HBM per device.

v0:
```python
import jax
import jax.numpy as jnp
from jax import lax
from jax.sharding import PartitionSpec as P

STEPS = 2
GAMMA = 1.4
TIME_STEP = 0.25
VISCOSITY = 0.15


def extended(block, sides, width):
    for axis, dim in sides:
        count = lax.axis_size(axis)
        forward = [(i, i + 1) for i in range(count - 1)]
        forward.append((count - 1, 0))
        backward = [(target, source) for source, target in forward]
        low = lax.ppermute(
            lax.slice_in_dim(block, block.shape[dim] - width, None, axis=dim), axis, forward
        )
        high = lax.ppermute(lax.slice_in_dim(block, 0, width, axis=dim), axis, backward)
        block = jnp.concatenate([low, block, high], axis=dim)
    return block


def flux_of(current, dim_index):
    density = current[0]
    momentum = current[1:4]
    energy = current[4]
    vel_d = momentum[dim_index] / density
    pressure = (GAMMA - 1.0) * (
        energy
        - 0.5
        * (momentum[0] * momentum[0] + momentum[1] * momentum[1] + momentum[2] * momentum[2])
        / density
    )
    components = [
        momentum[dim_index],
        momentum[0] * vel_d,
        momentum[1] * vel_d,
        momentum[2] * vel_d,
        (energy + pressure) * vel_d,
    ]
    components[1 + dim_index] = components[1 + dim_index] + pressure
    return jnp.stack(components)


def tendency(current):
    padded = extended(current.astype(jnp.bfloat16), (("wide", 1), ("narrow", 2)), 1).astype(
        current.dtype
    )
    flux_x = flux_of(padded[:, :, 1:-1], 0)
    flux_y = flux_of(padded[:, 1:-1, :], 1)
    flux_z = flux_of(current, 2)
    divergence = (
        flux_x[:, 2:]
        - flux_x[:, :-2]
        + (flux_y[:, :, 2:] - flux_y[:, :, :-2])
        + (jnp.roll(flux_z, -1, 3) - jnp.roll(flux_z, 1, 3))
    )
    laplace = (
        padded[:, 2:, 1:-1]
        + padded[:, :-2, 1:-1]
        + padded[:, 1:-1, 2:]
        + padded[:, 1:-1, :-2]
        + jnp.roll(current, -1, 3)
        + jnp.roll(current, 1, 3)
        - 6.0 * current
    )
    return -0.5 * divergence + VISCOSITY * laplace


def local(fields, prior_modes):
    wide_count = lax.axis_size("wide")
    narrow_count = lax.axis_size("narrow")
    cells_x, cells_y, cells_z = (fields.shape[1], fields.shape[2], fields.shape[3])
    inverse_cells = 1.0 / (cells_x * wide_count * cells_y * narrow_count * cells_z)
    flat_modes = prior_modes.reshape(prior_modes.shape[0], -1)
    contract = (((1,), (1,)), ((), ()))
    gram_modes = lax.dot_general(
        flat_modes, flat_modes, contract, preferred_element_type=jnp.float32
    )
    current = fields
    snapshots = []
    for step_index in range(STEPS):
        section_one = current + TIME_STEP * tendency(current)
        snapshots.append(section_one.astype(jnp.bfloat16))
        current = 0.5 * current + 0.5 * (section_one + TIME_STEP * tendency(section_one))
        snapshots.append(current.astype(jnp.bfloat16))
    arrived = lax.all_to_all(
        jnp.stack(snapshots), "narrow", split_axis=4, concat_axis=3, tiled=True
    )
    snap_rows = jnp.swapaxes(arrived, 3, 4).reshape(arrived.shape[0], -1)
    cross_gram = lax.dot_general(
        flat_modes, snap_rows, contract, preferred_element_type=jnp.float32
    )
    snap_gram = lax.dot_general(snap_rows, snap_rows, contract, preferred_element_type=jnp.float32)
    gram_local = jnp.concatenate(
        [
            jnp.concatenate([gram_modes, cross_gram], 1),
            jnp.concatenate([cross_gram.T, snap_gram], 1),
        ],
        0,
    )
    gram_local = gram_local * inverse_cells
    devices = wide_count * narrow_count
    everywhere = ("wide", "narrow")
    pieces = gram_local.reshape(devices, 1, -1)
    pieces = lax.all_to_all(pieces, everywhere, split_axis=0, concat_axis=0, tiled=True)
    piece = jnp.sum(pieces, axis=0, keepdims=True)
    copies = jnp.broadcast_to(piece, pieces.shape)
    copies = lax.all_to_all(copies, everywhere, split_axis=0, concat_axis=0, tiled=True)
    gram_whole = copies.reshape(gram_local.shape)
    factor = jnp.linalg.cholesky(gram_whole).T
    return (current, factor)


def solution(mesh):
    placed = (P(None, "wide", "narrow", None), P(None, None, "wide", "narrow"))
    return jax.shard_map(
        local,
        mesh=mesh,
        in_specs=placed,
        out_specs=(P(None, "wide", "narrow", None), P()),
        check_vma=False,
    )
```

profile of v0, /device:TPU:1, one launch (start us, length us, event | category | flops | bytes accessed | tf_op | source)
XLA Modules:
  0.0 132.0 jit_solution(1061865496528465805)
XLA Ops:
  0.6 0.8 convert_element_type.30
  1.4 1.4 %collective-permute-start.1 = (bf16[5,1,8,256]{3,2,1,0:T(8,128)(2,1)S(1)}, bf16[5,1,8,256]{3,2,1,0:T(8,128)(2,1)S(1)}, u32[]{:S(2)}, u32[]{:S(2)}) collective-permute-start(bf16[5,1,8,256]{3,2,1,0:T(8,128)(2,1)S(1)} %convert_element_type.30), channel_id=1, source_target_pairs={{8,0},{16,8},{24,16},{32,24},{40,32},{48,40},{56,48},{64,56},{72,6... | collective-permute-start | bytes 61448 | tf_op jit(solution)/shard_map/ppermute | solution.py:21
  2.8 1.6 %collective-permute-start = (bf16[5,1,8,256]{3,2,1,0:T(8,128)(2,1)S(1)}, bf16[5,1,8,256]{3,2,1,0:T(8,128)(2,1)S(1)}, u32[]{:S(2)}, u32[]{:S(2)}) collective-permute-start(bf16[5,1,8,256]{3,2,1,0:T(8,128)(2,1)S(1)} %convert_element_type.30), channel_id=1, source_target_pairs={{0,8},{8,16},{16,24},{24,32},{32,40},{40,48},{48,56},{56,64},{64,7... | collective-permute-start | bytes 61448 | tf_op jit(solution)/shard_map/ppermute | solution.py:18
  4.4 0.7 constant_dynamic-update-slice_fusion.14
  5.1 0.8 constant_dynamic-update-slice_fusion.13
  5.9 0.7 constant_dynamic-update-slice_fusion.12
  6.6 0.8 constant_dynamic-update-slice_fusion.11
  7.4 0.7 constant_dynamic-update-slice_fusion.10
  8.1 0.9 fusion.98
  9.1 5.2 %collective-permute-start.3 = (bf16[5,3,1,256]{3,1,2,0:T(4,128)(2,1)S(1)}, bf16[5,3,1,256]{3,1,2,0:T(4,128)(2,1)S(1)}, u32[]{:S(2)}, u32[]{:S(2)}) collective-permute-start(bf16[5,3,1,256]{3,1,2,0:T(4,128)(2,1)S(1)} %copy.436), channel_id=1, source_target_pairs={{1,0},{2,1},{3,2},{4,3},{5,4},{6,5},{7,6},{0,7},{9,8},{10,9},{11,1... | collective-permute-start | bytes 23048 | tf_op jit(solution)/shard_map/ppermute | solution.py:21
  14.3 0.8 fusion.99
  15.2 5.3 %collective-permute-done.2 = bf16[5,3,1,256]{3,1,2,0:T(4,128)(2,1)S(1)} collective-permute-done((bf16[5,3,1,256]{3,1,2,0:T(4,128)(2,1)S(1)}, bf16[5,3,1,256]{3,1,2,0:T(4,128)(2,1)S(1)}, u32[]{:S(2)}, u32[]{:S(2)}) %collective-permute-start.2) | collective-permute-done | bytes 7712 | tf_op jit(solution)/shard_map/ppermute | solution.py:18
  20.8 0.9 fusion.83
  21.6 4.9 %collective-permute-start.5 = (bf16[5,1,8,256]{3,2,0,1:T(8,128)(2,1)S(1)}, bf16[5,1,8,256]{3,2,0,1:T(8,128)(2,1)S(1)}, u32[]{:S(2)}, u32[]{:S(2)}) collective-permute-start(bf16[5,1,8,256]{3,2,0,1:T(8,128)(2,1)S(1)} %get-tuple-element.65), channel_id=1, source_target_pairs={{8,0},{16,8},{24,16},{32,24},{40,32},{48,40},{56,48},{64,56},{72,6... | collective-permute-start | bytes 61448 | tf_op jit(solution)/shard_map/ppermute | solution.py:21
  26.6 0.1 fusion.94
  26.8 0.6 collective-permute-done.5
  27.4 1.0 collective-permute-done.4
  28.4 0.7 collective-permute-start.7
  29.1 2.3 %collective-permute-start.6 = (bf16[5,3,1,256]{3,1,2,0:T(4,128)(2,1)S(1)}, bf16[5,3,1,256]{3,1,2,0:T(4,128)(2,1)S(1)}, u32[]{:S(2)}, u32[]{:S(2)}) collective-permute-start(bf16[5,3,1,256]{3,1,2,0:T(4,128)(2,1)S(1)} %copy.388), channel_id=1, source_target_pairs={{0,1},{1,2},{2,3},{3,4},{4,5},{5,6},{6,7},{7,0},{8,9},{9,10},{10,1... | collective-permute-start | bytes 23048 | tf_op jit(solution)/shard_map/ppermute | solution.py:18
  31.5 1.1 collective-permute-done.7
  32.6 2.6 %collective-permute-done.6 = bf16[5,3,1,256]{3,1,2,0:T(4,128)(2,1)S(1)} collective-permute-done((bf16[5,3,1,256]{3,1,2,0:T(4,128)(2,1)S(1)}, bf16[5,3,1,256]{3,1,2,0:T(4,128)(2,1)S(1)}, u32[]{:S(2)}, u32[]{:S(2)}) %collective-permute-start.6) | collective-permute-done | bytes 7712 | tf_op jit(solution)/shard_map/ppermute | solution.py:18
  35.5 0.1 broadcast_multiply_fusion
  35.7 0.1 fusion.92
  35.8 6.1 %collective-permute-start.9 = (bf16[5,1,8,256]{3,2,0,1:T(8,128)(2,1)S(1)}, bf16[5,1,8,256]{3,2,0,1:T(8,128)(2,1)S(1)}, u32[]{:S(2)}, u32[]{:S(2)}) collective-permute-start(bf16[5,1,8,256]{3,2,0,1:T(8,128)(2,1)S(1)} %fusion.78), channel_id=1, source_target_pairs={{8,0},{16,8},{24,16},{32,24},{40,32},{48,40},{56,48},{64,56},{72,6... | collective-permute-start | bytes 61448 | tf_op jit(solution)/shard_map/ppermute | solution.py:21
  42.0 0.1 fusion.90
  42.1 0.6 collective-permute-done.9
  42.8 0.3 collective-permute-done.8
  43.2 0.1 collective-permute-start.11
  43.3 2.9 %collective-permute-start.10 = (bf16[5,3,1,256]{3,1,2,0:T(4,128)(2,1)S(1)}, bf16[5,3,1,256]{3,1,2,0:T(4,128)(2,1)S(1)}, u32[]{:S(2)}, u32[]{:S(2)}) collective-permute-start(bf16[5,3,1,256]{3,1,2,0:T(4,128)(2,1)S(1)} %copy.400), channel_id=1, source_target_pairs={{0,1},{1,2},{2,3},{3,4},{4,5},{5,6},{6,7},{7,0},{8,9},{9,10},{10,1... | collective-permute-start | bytes 23048 | tf_op jit(solution)/shard_map/ppermute | solution.py:18
  46.2 1.0 collective-permute-done.11
  47.3 2.2 %collective-permute-done.10 = bf16[5,3,1,256]{3,1,2,0:T(4,128)(2,1)S(1)} collective-permute-done((bf16[5,3,1,256]{3,1,2,0:T(4,128)(2,1)S(1)}, bf16[5,3,1,256]{3,1,2,0:T(4,128)(2,1)S(1)}, u32[]{:S(2)}, u32[]{:S(2)}) %collective-permute-start.10) | collective-permute-done | bytes 7712 | tf_op jit(solution)/shard_map/ppermute | solution.py:18
  49.8 0.1 fusion.80
  49.9 5.4 %collective-permute-start.13 = (bf16[5,1,8,256]{3,2,0,1:T(8,128)(2,1)S(1)}, bf16[5,1,8,256]{3,2,0,1:T(8,128)(2,1)S(1)}, u32[]{:S(2)}, u32[]{:S(2)}) collective-permute-start(bf16[5,1,8,256]{3,2,0,1:T(8,128)(2,1)S(1)} %get-tuple-element.31), channel_id=1, source_target_pairs={{8,0},{16,8},{24,16},{32,24},{40,32},{48,40},{56,48},{64,56},{72,6... | collective-permute-start | bytes 61448 | tf_op jit(solution)/shard_map/ppermute | solution.py:21
  55.5 0.1 fusion.86
  55.6 0.6 collective-permute-done.13
  56.2 0.3 collective-permute-done.12
  56.6 0.1 collective-permute-start.15
  56.7 2.9 %collective-permute-start.14 = (bf16[5,3,1,256]{3,1,2,0:T(4,128)(2,1)S(1)}, bf16[5,3,1,256]{3,1,2,0:T(4,128)(2,1)S(1)}, u32[]{:S(2)}, u32[]{:S(2)}) collective-permute-start(bf16[5,3,1,256]{3,1,2,0:T(4,128)(2,1)S(1)} %copy.411), channel_id=1, source_target_pairs={{0,1},{1,2},{2,3},{3,4},{4,5},{5,6},{6,7},{7,0},{8,9},{9,10},{10,1... | collective-permute-start | bytes 23048 | tf_op jit(solution)/shard_map/ppermute | solution.py:18
  59.7 1.0 collective-permute-done.15
  60.7 2.2 %collective-permute-done.14 = bf16[5,3,1,256]{3,1,2,0:T(4,128)(2,1)S(1)} collective-permute-done((bf16[5,3,1,256]{3,1,2,0:T(4,128)(2,1)S(1)}, bf16[5,3,1,256]{3,1,2,0:T(4,128)(2,1)S(1)}, u32[]{:S(2)}, u32[]{:S(2)}) %collective-permute-start.14) | collective-permute-done | bytes 7712 | tf_op jit(solution)/shard_map/ppermute | solution.py:18
  63.2 0.7 convert_bitcast_fusion
  63.9 0.7 copy.422
  64.7 2.0 %reshape.669 = bf16[8,2,2560]{2,1,0:T(2,128)(2,1)} reshape(bf16[256,5,1,4,8]{4,3,2,1,0:T(4,128)(2,1)S(1)} %bitcast.162) | data formatting | bytes 163840
  66.7 3.5 %all-to-all-start = ((bf16[8,2,2560]{2,1,0:T(2,128)(2,1)}), bf16[8,2,2560]{2,1,0:T(2,128)(2,1)S(1)}, u32[]{:S(2)}, u32[]{:S(2)}) async-start(bf16[8,2,2560]{2,1,0:T(2,128)(2,1)} %reshape.669), calls=%async_computation | async-start | bytes 163840 | tf_op jit(solution)/shard_map/all_to_all | solution.py:90
  70.2 3.4 %fusion.2 = f32[124,124]{0,1:T(8,128)S(1)} fusion(bf16[124,5,1,2048]{3,0,2,1:T(8,128)(2,1)} %param.3), kind=kOutput, calls=%fused_computation.2 | convolution fusion | flops 314900480 | bytes 2601024 | tf_op jit(solution)/shard_map/dot_general | solution.py:80
  73.6 3.3 %copy.426 = bf16[124,5,1,2048]{0,3,1,2:T(8,128)(2,1)S(1)} copy(bf16[124,5,1,2048]{3,0,2,1:T(8,128)(2,1)} %param.3) | data formatting | bytes 5079040 | tf_op args[1]
  76.9 2.6 %reshape.670 = bf16[256,5,1,4,8]{4,3,2,1,0:T(4,128)(2,1)} reshape(bf16[8,2,2560]{2,1,0:T(2,128)(2,1)S(1)} %all-to-all-done) | data formatting | bytes 163840
  79.5 1.8 %copy.423 = bf16[4,5,1,8,8,32]{5,3,4,1,0,2:T(8,128)(2,1)S(1)} copy(bf16[4,5,1,8,8,32]{3,0,1,5,4,2:T(4,128)(2,1)} %bitcast.163) | data formatting | bytes 163840 | tf_op jit(solution)/shard_map/all_to_all | solution.py:90
  81.4 0.2 copy.424
  81.6 0.3 convolution_bitcast_fusion
  81.9 0.2 reshape.663
  82.0 0.4 fusion.102
  82.5 0.1 pad_maximum_fusion.31
  82.6 0.1 copy.427
  82.7 0.1 maximum_multiply_fusion
  82.8 0.1 copy.428
  82.9 21.2 %all_to_all.28 = f32[128,1,128]{2,1,0:T(1,128)S(1)} all-to-all(f32[128,1,128]{2,1,0:T(1,128)S(1)} %copy.428), channel_id=1, replica_groups=mesh['wide'=16,'narrow'=8] {'wide','narrow'}, dimensions={0} | all-to-all | bytes 131072 | tf_op jit(solution)/shard_map/all_to_all | solution.py:109
  104.1 0.2 reduce_sum.9
  104.3 13.8 %all_to_all.29 = f32[128,1,128]{2,1,0:T(1,128)S(1)} all-to-all(f32[128,1,128]{2,1,0:T(1,128)S(1)} %broadcast_in_dim.3), channel_id=1, replica_groups=mesh['wide'=16,'narrow'=8] {'wide','narrow'}, dimensions={0} | all-to-all | bytes 131072 | tf_op jit(solution)/shard_map/all_to_all | solution.py:112
  118.1 0.1 copy.429
  118.2 11.7 %cholesky.18 = f32[128,128]{1,0:T(8,128)S(1)} custom-call(f32[128,128]{1,0:T(8,128)S(1)} %fusion.6), custom_call_target="Cholesky" | custom-call | tf_op jit(solution)/shard_map/jit(cholesky)/cholesky | solution.py:114
  130.0 0.6 compare_reduce_fusion
  130.6 0.7 select_bitcast_fusion
  131.3 0.7 copy.432
  (106 shorter events, 2.0 us)
Async XLA Ops:
  1.4 7.6 %collective-permute-start.1 = (bf16[5,1,8,256]{3,2,1,0:T(8,128)(2,1)S(1)}, bf16[5,1,8,256]{3,2,1,0:T(8,128)(2,1)S(1)}, u32[]{:S(2)}, u32[]{:S(2)}) collective-permute-start(bf16[5,1,8,256]{3,2,1,0:T(8,128)(2,1)S(1)} %convert_element_type.30), channel_id=1, source_target_pairs={{8,0},{16,8},{24,16},{32,24},{40,32},{48,40},{56,48},{64,56},{72,6... | collective-permute-start | bytes 61448 | tf_op jit(solution)/shard_map/ppermute | solution.py:21
  2.8 6.3 %collective-permute-start = (bf16[5,1,8,256]{3,2,1,0:T(8,128)(2,1)S(1)}, bf16[5,1,8,256]{3,2,1,0:T(8,128)(2,1)S(1)}, u32[]{:S(2)}, u32[]{:S(2)}) collective-permute-start(bf16[5,1,8,256]{3,2,1,0:T(8,128)(2,1)S(1)} %convert_element_type.30), channel_id=1, source_target_pairs={{0,8},{8,16},{16,24},{24,32},{32,40},{40,48},{48,56},{56,64},{64,7... | collective-permute-start | bytes 61448 | tf_op jit(solution)/shard_map/ppermute | solution.py:18
  5.1 30.4 %copy-start = (f32[5,1,8,256]{3,2,1,0:T(8,128)S(1)}, f32[5,1,8,256]{3,2,1,0:T(8,128)}, u32[]{:S(2)}) copy-start(f32[5,1,8,256]{3,2,1,0:T(8,128)} %param.2) | copy-start | bytes 122884
  9.1 6.0 %collective-permute-start.3 = (bf16[5,3,1,256]{3,1,2,0:T(4,128)(2,1)S(1)}, bf16[5,3,1,256]{3,1,2,0:T(4,128)(2,1)S(1)}, u32[]{:S(2)}, u32[]{:S(2)}) collective-permute-start(bf16[5,3,1,256]{3,1,2,0:T(4,128)(2,1)S(1)} %copy.436), channel_id=1, source_target_pairs={{1,0},{2,1},{3,2},{4,3},{5,4},{6,5},{7,6},{0,7},{9,8},{10,9},{11,1... | collective-permute-start | bytes 23048 | tf_op jit(solution)/shard_map/ppermute | solution.py:21
  14.3 6.1 %collective-permute-start.2 = (bf16[5,3,1,256]{3,1,2,0:T(4,128)(2,1)S(1)}, bf16[5,3,1,256]{3,1,2,0:T(4,128)(2,1)S(1)}, u32[]{:S(2)}, u32[]{:S(2)}) collective-permute-start(bf16[5,3,1,256]{3,1,2,0:T(4,128)(2,1)S(1)} %copy.435), channel_id=1, source_target_pairs={{0,1},{1,2},{2,3},{3,4},{4,5},{5,6},{6,7},{7,0},{8,9},{9,10},{10,1... | collective-permute-start | bytes 23048 | tf_op jit(solution)/shard_map/ppermute | solution.py:18
  21.6 5.7 %collective-permute-start.5 = (bf16[5,1,8,256]{3,2,0,1:T(8,128)(2,1)S(1)}, bf16[5,1,8,256]{3,2,0,1:T(8,128)(2,1)S(1)}, u32[]{:S(2)}, u32[]{:S(2)}) collective-permute-start(bf16[5,1,8,256]{3,2,0,1:T(8,128)(2,1)S(1)} %get-tuple-element.65), channel_id=1, source_target_pairs={{8,0},{16,8},{24,16},{32,24},{40,32},{48,40},{56,48},{64,56},{72,6... | collective-permute-start | bytes 61448 | tf_op jit(solution)/shard_map/ppermute | solution.py:21
  26.5 1.8 %collective-permute-start.4 = (bf16[5,1,8,256]{3,2,0,1:T(8,128)(2,1)S(1)}, bf16[5,1,8,256]{3,2,0,1:T(8,128)(2,1)S(1)}, u32[]{:S(2)}, u32[]{:S(2)}) collective-permute-start(bf16[5,1,8,256]{3,2,0,1:T(8,128)(2,1)S(1)} %get-tuple-element.65), channel_id=1, source_target_pairs={{0,8},{8,16},{16,24},{24,32},{32,40},{40,48},{48,56},{56,64},{64,7... | collective-permute-start | bytes 61448 | tf_op jit(solution)/shard_map/ppermute | solution.py:18
  28.4 4.2 %collective-permute-start.7 = (bf16[5,3,1,256]{3,1,2,0:T(4,128)(2,1)S(1)}, bf16[5,3,1,256]{3,1,2,0:T(4,128)(2,1)S(1)}, u32[]{:S(2)}, u32[]{:S(2)}) collective-permute-start(bf16[5,3,1,256]{3,1,2,0:T(4,128)(2,1)S(1)} %copy.389), channel_id=1, source_target_pairs={{1,0},{2,1},{3,2},{4,3},{5,4},{6,5},{7,6},{0,7},{9,8},{10,9},{11,1... | collective-permute-start | bytes 23048 | tf_op jit(solution)/shard_map/ppermute | solution.py:21
  29.1 6.1 %collective-permute-start.6 = (bf16[5,3,1,256]{3,1,2,0:T(4,128)(2,1)S(1)}, bf16[5,3,1,256]{3,1,2,0:T(4,128)(2,1)S(1)}, u32[]{:S(2)}, u32[]{:S(2)}) collective-permute-start(bf16[5,3,1,256]{3,1,2,0:T(4,128)(2,1)S(1)} %copy.388), channel_id=1, source_target_pairs={{0,1},{1,2},{2,3},{3,4},{4,5},{5,6},{6,7},{7,0},{8,9},{9,10},{10,1... | collective-permute-start | bytes 23048 | tf_op jit(solution)/shard_map/ppermute | solution.py:18
  35.8 7.0 %collective-permute-start.9 = (bf16[5,1,8,256]{3,2,0,1:T(8,128)(2,1)S(1)}, bf16[5,1,8,256]{3,2,0,1:T(8,128)(2,1)S(1)}, u32[]{:S(2)}, u32[]{:S(2)}) collective-permute-start(bf16[5,1,8,256]{3,2,0,1:T(8,128)(2,1)S(1)} %fusion.78), channel_id=1, source_target_pairs={{8,0},{16,8},{24,16},{32,24},{40,32},{48,40},{56,48},{64,56},{72,6... | collective-permute-start | bytes 61448 | tf_op jit(solution)/shard_map/ppermute | solution.py:21
  41.9 1.2 collective-permute-start.8
  43.2 4.1 %collective-permute-start.11 = (bf16[5,3,1,256]{3,1,2,0:T(4,128)(2,1)S(1)}, bf16[5,3,1,256]{3,1,2,0:T(4,128)(2,1)S(1)}, u32[]{:S(2)}, u32[]{:S(2)}) collective-permute-start(bf16[5,3,1,256]{3,1,2,0:T(4,128)(2,1)S(1)} %copy.401), channel_id=1, source_target_pairs={{1,0},{2,1},{3,2},{4,3},{5,4},{6,5},{7,6},{0,7},{9,8},{10,9},{11,1... | collective-permute-start | bytes 23048 | tf_op jit(solution)/shard_map/ppermute | solution.py:21
  43.3 6.2 %collective-permute-start.10 = (bf16[5,3,1,256]{3,1,2,0:T(4,128)(2,1)S(1)}, bf16[5,3,1,256]{3,1,2,0:T(4,128)(2,1)S(1)}, u32[]{:S(2)}, u32[]{:S(2)}) collective-permute-start(bf16[5,3,1,256]{3,1,2,0:T(4,128)(2,1)S(1)} %copy.400), channel_id=1, source_target_pairs={{0,1},{1,2},{2,3},{3,4},{4,5},{5,6},{6,7},{7,0},{8,9},{9,10},{10,1... | collective-permute-start | bytes 23048 | tf_op jit(solution)/shard_map/ppermute | solution.py:18
  49.9 6.3 %collective-permute-start.13 = (bf16[5,1,8,256]{3,2,0,1:T(8,128)(2,1)S(1)}, bf16[5,1,8,256]{3,2,0,1:T(8,128)(2,1)S(1)}, u32[]{:S(2)}, u32[]{:S(2)}) collective-permute-start(bf16[5,1,8,256]{3,2,0,1:T(8,128)(2,1)S(1)} %get-tuple-element.31), channel_id=1, source_target_pairs={{8,0},{16,8},{24,16},{32,24},{40,32},{48,40},{56,48},{64,56},{72,6... | collective-permute-start | bytes 61448 | tf_op jit(solution)/shard_map/ppermute | solution.py:21
  55.3 1.2 collective-permute-start.12
  56.6 4.1 %collective-permute-start.15 = (bf16[5,3,1,256]{3,1,2,0:T(4,128)(2,1)S(1)}, bf16[5,3,1,256]{3,1,2,0:T(4,128)(2,1)S(1)}, u32[]{:S(2)}, u32[]{:S(2)}) collective-permute-start(bf16[5,3,1,256]{3,1,2,0:T(4,128)(2,1)S(1)} %copy.412), channel_id=1, source_target_pairs={{1,0},{2,1},{3,2},{4,3},{5,4},{6,5},{7,6},{0,7},{9,8},{10,9},{11,1... | collective-permute-start | bytes 23048 | tf_op jit(solution)/shard_map/ppermute | solution.py:21
  56.7 6.2 %collective-permute-start.14 = (bf16[5,3,1,256]{3,1,2,0:T(4,128)(2,1)S(1)}, bf16[5,3,1,256]{3,1,2,0:T(4,128)(2,1)S(1)}, u32[]{:S(2)}, u32[]{:S(2)}) collective-permute-start(bf16[5,3,1,256]{3,1,2,0:T(4,128)(2,1)S(1)} %copy.411), channel_id=1, source_target_pairs={{0,1},{1,2},{2,3},{3,4},{4,5},{5,6},{6,7},{7,0},{8,9},{9,10},{10,1... | collective-permute-start | bytes 23048 | tf_op jit(solution)/shard_map/ppermute | solution.py:18
  66.7 10.2 %all-to-all-start = ((bf16[8,2,2560]{2,1,0:T(2,128)(2,1)}), bf16[8,2,2560]{2,1,0:T(2,128)(2,1)S(1)}, u32[]{:S(2)}, u32[]{:S(2)}) async-start(bf16[8,2,2560]{2,1,0:T(2,128)(2,1)} %reshape.669), calls=%async_computation | async-start | bytes 163840 | tf_op jit(solution)/shard_map/all_to_all | solution.py:90
where the time goes:
time: 133 us; the launch traced here: 132 us
  starting transfers between devices  37.2 us (28%)
  blocking collectives  35 us (26%)
  other arithmetic  20.1 us (15%)
  waiting for transfers between devices  18.8 us (14%)
  local copies, waits for them, and re-layouts  15.5 us (12%)
  matrix products  4.09 us (3%)
    ppermute x8, starting transfers between devices, extended(): lax.ppermute(lax.slice_in_dim(block, 0, width, axis=dim), axis, backward)  23.8 us
    all_to_all x1, blocking collectives, local(): lax.all_to_all(pieces, everywhere, split_axis=0, concat_axis=0, tiled=True)  21.2 us
    ppermute x8, waiting for transfers between devices, extended(): lax.ppermute(lax.slice_in_dim(block, block.shape[dim] - width, None, axis...  13.9 us
    all_to_all x1, blocking collectives, local(): lax.all_to_all(copies, everywhere, split_axis=0, concat_axis=0, tiled=True)  13.8 us
    another operation x3, other arithmetic, local(): factor = jnp.linalg.cholesky(gram_whole).T  12.4 us
    ppermute x8, starting transfers between devices, extended(): lax.ppermute(lax.slice_in_dim(block, block.shape[dim] - width, None, axis...  9.89 us
    unnamed x16, local copies, waits for them, and re-layouts  9.42 us
    ppermute x8, waiting for transfers between devices, extended(): lax.ppermute(lax.slice_in_dim(block, 0, width, axis=dim), axis, backward)  4.85 us
  transfers between devices with their start and end apart: 17, of which 13 were waited for; matrix products, arithmetic and copies ran while one was open for 10% of the time, Pallas kernels for 0%

commit v1 on v0

--- a/solution.py
+++ b/solution.py
@@ -87,9 +87,11 @@
         snapshots.append(section_one.astype(jnp.bfloat16))
         current = 0.5 * current + 0.5 * (section_one + TIME_STEP * tendency(section_one))
         snapshots.append(current.astype(jnp.bfloat16))
-    arrived = lax.all_to_all(
-        jnp.stack(snapshots), "narrow", split_axis=4, concat_axis=3, tiled=True
-    )
+    x = jnp.stack(snapshots)
+    size = lax.axis_size("narrow")
+    blocks = jnp.stack(jnp.split(x, size, axis=4), axis=0)
+    blocks = lax.all_to_all(blocks, "narrow", split_axis=0, concat_axis=0)
+    arrived = jnp.concatenate(blocks, axis=3)
     snap_rows = jnp.swapaxes(arrived, 3, 4).reshape(arrived.shape[0], -1)
     cross_gram = lax.dot_general(
         flat_modes, snap_rows, contract, preferred_element_type=jnp.float32

time: 133 us -> 125 us (0.940)
  local copies, waits for them, and re-layouts: 15.5 us -> 9.92 us
  waiting for transfers between devices: 18.8 us -> 21.4 us
  matrix products: 4.09 us -> 1.55 us
  blocking collectives: 35 us -> 32.8 us
    unnamed x16 -> x23, local copies, waits for them, and re-layouts: 9.42 us -> 6.39 us
    dot_general x1, matrix products: 3.37 us -> 0.84 us  [local(): lax.dot_general(flat_modes, flat_modes, contract, preferred_element_type=...]
    all_to_all x1, waiting for transfers between devices: 0.01 us -> 2.4 us  [local(): blocks = lax.all_to_all(blocks, 'narrow', split_axis=0, concat_axis=0)]
    all_to_all x1, blocking collectives: 21.2 us -> 19.1 us  [local(): lax.all_to_all(pieces, everywhere, split_axis=0, concat_axis=0, tiled=True)]
    all_to_all x2 -> x0, local copies, waits for them, and re-layouts: 2 us -> none  [local(): lax.all_to_all(jnp.stack(snapshots), 'narrow', split_axis=4, concat_axis=...]
  transfers between devices with their start and end apart: 17 -> 17, of which waited for: 13 -> 14; matrix products, arithmetic and copies ran while one was open for 10% -> 8% of each run, Pallas kernels for 0% -> 0%
where the time goes in v1:
time: 125 us; the launch traced here: 124 us
  starting transfers between devices  37.1 us (30%)
  blocking collectives  32.8 us (26%)
  waiting for transfers between devices  21.4 us (17%)
  other arithmetic  20.1 us (16%)
  local copies, waits for them, and re-layouts  9.92 us (8%)
  matrix products  1.55 us (1%)
  between operations  1.25 us (1%)
    ppermute x8, starting transfers between devices, extended(): lax.ppermute(lax.slice_in_dim(block, 0, width, axis=dim), axis, backward)  23.8 us
    all_to_all x1, blocking collectives, local(): lax.all_to_all(pieces, everywhere, split_axis=0, concat_axis=0, tiled=True)  19.1 us
    ppermute x8, waiting for transfers between devices, extended(): lax.ppermute(lax.slice_in_dim(block, block.shape[dim] - width, None, axis...  14 us
    all_to_all x1, blocking collectives, local(): lax.all_to_all(copies, everywhere, split_axis=0, concat_axis=0, tiled=True)  13.8 us
    another operation x3, other arithmetic, local(): factor = jnp.linalg.cholesky(gram_whole).T  12.4 us
    ppermute x8, starting transfers between devices, extended(): lax.ppermute(lax.slice_in_dim(block, block.shape[dim] - width, None, axis...  9.92 us
    unnamed x23, local copies, waits for them, and re-layouts  6.39 us
    ppermute x8, waiting for transfers between devices, extended(): lax.ppermute(lax.slice_in_dim(block, 0, width, axis=dim), axis, backward)  5.03 us
  transfers between devices with their start and end apart: 17, of which 14 were waited for; matrix products, arithmetic and copies ran while one was open for 8% of the time, Pallas kernels for 0%

profile of v1, /device:TPU:1, one launch (start us, length us, event | category | flops | bytes accessed | tf_op | source)
XLA Modules:
  0.0 124.2 jit_solution(17621525473806025044)
XLA Ops:
  0.6 0.8 bitcast_convert_fusion
  1.5 1.4 %collective-permute-start.1 = (bf16[5,1,8,256]{3,2,0,1:T(8,128)(2,1)S(1)}, bf16[5,1,8,256]{3,2,0,1:T(8,128)(2,1)S(1)}, u32[]{:S(2)}, u32[]{:S(2)}) collective-permute-start(bf16[5,1,8,256]{3,2,0,1:T(8,128)(2,1)S(1)} %bitcast_convert_fusion), channel_id=1, source_target_pairs={{8,0},{16,8},{24,16},{32,24},{40,32},{48,40},{56,48},{64,56},{72,6... | collective-permute-start | bytes 61448 | tf_op jit(solution)/shard_map/ppermute | solution.py:21
  2.9 1.6 %collective-permute-start = (bf16[5,1,8,256]{3,2,0,1:T(8,128)(2,1)S(1)}, bf16[5,1,8,256]{3,2,0,1:T(8,128)(2,1)S(1)}, u32[]{:S(2)}, u32[]{:S(2)}) collective-permute-start(bf16[5,1,8,256]{3,2,0,1:T(8,128)(2,1)S(1)} %bitcast_convert_fusion), channel_id=1, source_target_pairs={{0,8},{8,16},{16,24},{24,32},{32,40},{40,48},{48,56},{56,64},{64,7... | collective-permute-start | bytes 61448 | tf_op jit(solution)/shard_map/ppermute | solution.py:18
  4.5 0.7 constant_dynamic-update-slice_fusion.14
  5.2 0.7 constant_dynamic-update-slice_fusion.13
  5.9 0.7 constant_dynamic-update-slice_fusion.12
  6.6 0.8 constant_dynamic-update-slice_fusion.11
  7.4 0.7 constant_dynamic-update-slice_fusion.10
  8.1 0.9 fusion.95
  9.1 5.2 %collective-permute-start.3 = (bf16[5,3,1,256]{3,2,0,1:T(2,128)(2,1)S(1)}, bf16[5,3,1,256]{3,2,0,1:T(2,128)(2,1)S(1)}, u32[]{:S(2)}, u32[]{:S(2)}) collective-permute-start(bf16[5,3,1,256]{3,2,0,1:T(2,128)(2,1)S(1)} %get-tuple-element.85), channel_id=1, source_target_pairs={{1,0},{2,1},{3,2},{4,3},{5,4},{6,5},{7,6},{0,7},{9,8},{10,9},{11,1... | collective-permute-start | bytes 23048 | tf_op jit(solution)/shard_map/ppermute | solution.py:21
  14.3 0.8 fusion.96
  15.2 5.3 %collective-permute-done.2 = bf16[5,3,1,256]{3,2,0,1:T(2,128)(2,1)S(1)} collective-permute-done((bf16[5,3,1,256]{3,2,0,1:T(2,128)(2,1)S(1)}, bf16[5,3,1,256]{3,2,0,1:T(2,128)(2,1)S(1)}, u32[]{:S(2)}, u32[]{:S(2)}) %collective-permute-start.2) | collective-permute-done | bytes 7712 | tf_op jit(solution)/shard_map/ppermute | solution.py:18
  20.8 0.9 fusion.81
  21.7 4.9 %collective-permute-start.5 = (bf16[5,1,8,256]{3,2,0,1:T(8,128)(2,1)S(1)}, bf16[5,1,8,256]{3,2,0,1:T(8,128)(2,1)S(1)}, u32[]{:S(2)}, u32[]{:S(2)}) collective-permute-start(bf16[5,1,8,256]{3,2,0,1:T(8,128)(2,1)S(1)} %get-tuple-element.59), channel_id=1, source_target_pairs={{8,0},{16,8},{24,16},{32,24},{40,32},{48,40},{56,48},{64,56},{72,6... | collective-permute-start | bytes 61448 | tf_op jit(solution)/shard_map/ppermute | solution.py:21
  26.9 0.6 collective-permute-done.5
  27.4 0.9 collective-permute-done.4
  28.4 0.7 collective-permute-start.7
  29.1 2.4 %collective-permute-start.6 = (bf16[5,3,1,256]{3,2,0,1:T(2,128)(2,1)S(1)}, bf16[5,3,1,256]{3,2,0,1:T(2,128)(2,1)S(1)}, u32[]{:S(2)}, u32[]{:S(2)}) collective-permute-start(bf16[5,3,1,256]{3,2,0,1:T(2,128)(2,1)S(1)} %get-tuple-element.82), channel_id=1, source_target_pairs={{0,1},{1,2},{2,3},{3,4},{4,5},{5,6},{6,7},{7,0},{8,9},{9,10},{10,1... | collective-permute-start | bytes 23048 | tf_op jit(solution)/shard_map/ppermute | solution.py:18
  31.5 1.1 collective-permute-done.7
  32.6 2.7 %collective-permute-done.6 = bf16[5,3,1,256]{3,2,0,1:T(2,128)(2,1)S(1)} collective-permute-done((bf16[5,3,1,256]{3,2,0,1:T(2,128)(2,1)S(1)}, bf16[5,3,1,256]{3,2,0,1:T(2,128)(2,1)S(1)}, u32[]{:S(2)}, u32[]{:S(2)}) %collective-permute-start.6) | collective-permute-done | bytes 7712 | tf_op jit(solution)/shard_map/ppermute | solution.py:18
  35.5 0.1 broadcast_multiply_fusion
  35.8 6.1 %collective-permute-start.9 = (bf16[5,1,8,256]{3,2,0,1:T(8,128)(2,1)S(1)}, bf16[5,1,8,256]{3,2,0,1:T(8,128)(2,1)S(1)}, u32[]{:S(2)}, u32[]{:S(2)}) collective-permute-start(bf16[5,1,8,256]{3,2,0,1:T(8,128)(2,1)S(1)} %fusion.75), channel_id=1, source_target_pairs={{8,0},{16,8},{24,16},{32,24},{40,32},{48,40},{56,48},{64,56},{72,6... | collective-permute-start | bytes 61448 | tf_op jit(solution)/shard_map/ppermute | solution.py:21
  42.2 0.6 collective-permute-done.9
  42.8 0.3 collective-permute-done.8
  43.2 3.0 %collective-permute-start.10 = (bf16[5,3,1,256]{3,2,0,1:T(2,128)(2,1)S(1)}, bf16[5,3,1,256]{3,2,0,1:T(2,128)(2,1)S(1)}, u32[]{:S(2)}, u32[]{:S(2)}) collective-permute-start(bf16[5,3,1,256]{3,2,0,1:T(2,128)(2,1)S(1)} %get-tuple-element.80), channel_id=1, source_target_pairs={{0,1},{1,2},{2,3},{3,4},{4,5},{5,6},{6,7},{7,0},{8,9},{9,10},{10,1... | collective-permute-start | bytes 23048 | tf_op jit(solution)/shard_map/ppermute | solution.py:18
  46.2 1.1 collective-permute-done.11
  47.3 2.2 %collective-permute-done.10 = bf16[5,3,1,256]{3,2,0,1:T(2,128)(2,1)S(1)} collective-permute-done((bf16[5,3,1,256]{3,2,0,1:T(2,128)(2,1)S(1)}, bf16[5,3,1,256]{3,2,0,1:T(2,128)(2,1)S(1)}, u32[]{:S(2)}, u32[]{:S(2)}) %collective-permute-start.10) | collective-permute-done | bytes 7712 | tf_op jit(solution)/shard_map/ppermute | solution.py:18
  49.8 0.1 fusion.78
  49.9 5.4 %collective-permute-start.13 = (bf16[5,1,8,256]{3,2,0,1:T(8,128)(2,1)S(1)}, bf16[5,1,8,256]{3,2,0,1:T(8,128)(2,1)S(1)}, u32[]{:S(2)}, u32[]{:S(2)}) collective-permute-start(bf16[5,1,8,256]{3,2,0,1:T(8,128)(2,1)S(1)} %get-tuple-element.25), channel_id=1, source_target_pairs={{8,0},{16,8},{24,16},{32,24},{40,32},{48,40},{56,48},{64,56},{72,6... | collective-permute-start | bytes 61448 | tf_op jit(solution)/shard_map/ppermute | solution.py:21
  55.6 0.6 collective-permute-done.13
  56.2 0.3 collective-permute-done.12
  56.7 3.0 %collective-permute-start.14 = (bf16[5,3,1,256]{3,2,0,1:T(2,128)(2,1)S(1)}, bf16[5,3,1,256]{3,2,0,1:T(2,128)(2,1)S(1)}, u32[]{:S(2)}, u32[]{:S(2)}) collective-permute-start(bf16[5,3,1,256]{3,2,0,1:T(2,128)(2,1)S(1)} %get-tuple-element.78), channel_id=1, source_target_pairs={{0,1},{1,2},{2,3},{3,4},{4,5},{5,6},{6,7},{7,0},{8,9},{9,10},{10,1... | collective-permute-start | bytes 23048 | tf_op jit(solution)/shard_map/ppermute | solution.py:18
  59.7 1.0 collective-permute-done.15
  60.7 2.2 %collective-permute-done.14 = bf16[5,3,1,256]{3,2,0,1:T(2,128)(2,1)S(1)} collective-permute-done((bf16[5,3,1,256]{3,2,0,1:T(2,128)(2,1)S(1)}, bf16[5,3,1,256]{3,2,0,1:T(2,128)(2,1)S(1)}, u32[]{:S(2)}, u32[]{:S(2)}) %collective-permute-start.14) | collective-permute-done | bytes 7712 | tf_op jit(solution)/shard_map/ppermute | solution.py:18
  63.2 0.7 convert_bitcast_fusion
  64.0 0.1 constant_dynamic-update-slice_fusion.66
  64.1 0.1 constant_dynamic-update-slice_fusion.65
  64.2 0.1 constant_dynamic-update-slice_fusion.64
  64.3 0.1 constant_dynamic-update-slice_fusion.62
  64.4 0.1 constant_dynamic-update-slice_fusion.61
  64.5 0.1 constant_dynamic-update-slice_fusion.60
  64.6 0.9 reshape.677
  65.5 3.4 %all-to-all-start = ((bf16[8,2,2560]{2,1,0:T(2,128)(2,1)}), bf16[8,2,2560]{2,1,0:T(2,128)(2,1)S(1)}, u32[]{:S(2)}, u32[]{:S(2)}) async-start(bf16[8,2,2560]{2,1,0:T(2,128)(2,1)} %reshape.677), calls=%async_computation | async-start | bytes 163840 | tf_op jit(solution)/shard_map/all_to_all | solution.py:93
  68.9 0.8 fusion.2
  69.7 3.3 %copy.86 = bf16[124,5,1,2048]{0,3,1,2:T(8,128)(2,1)S(1)} copy(bf16[124,5,1,2048]{3,0,2,1:T(8,128)(2,1)} %param.3) | data formatting | bytes 5079040 | tf_op args[1]
  73.0 2.4 %all-to-all-done = bf16[8,2,2560]{2,1,0:T(2,128)(2,1)S(1)} async-done(((bf16[8,2,2560]{2,1,0:T(2,128)(2,1)}), bf16[8,2,2560]{2,1,0:T(2,128)(2,1)S(1)}, u32[]{:S(2)}, u32[]{:S(2)}) %all-to-all-start) | async-done | bytes 81952 | tf_op jit(solution)/shard_map/all_to_all | solution.py:93
  75.4 0.2 reshape.678
  75.6 0.1 copy_bitcast_fusion
  75.7 0.2 copy.84
  75.9 0.3 convolution_bitcast_fusion
  76.3 0.2 reshape.671
  76.4 0.4 fusion.99
  76.9 0.1 pad_maximum_fusion.33
  76.9 0.1 copy.87
  77.1 0.1 maximum_multiply_fusion
  77.2 0.1 copy.88
  77.3 19.1 %all_to_all.15 = f32[128,1,128]{2,1,0:T(1,128)S(1)} all-to-all(f32[128,1,128]{2,1,0:T(1,128)S(1)} %copy.88), channel_id=1, replica_groups=mesh['wide'=16,'narrow'=8] {'wide','narrow'}, dimensions={0} | all-to-all | bytes 131072 | tf_op jit(solution)/shard_map/all_to_all | solution.py:111
  96.3 0.2 reduce_sum.9
  96.5 13.8 %all_to_all.16 = f32[128,1,128]{2,1,0:T(1,128)S(1)} all-to-all(f32[128,1,128]{2,1,0:T(1,128)S(1)} %broadcast_in_dim.3), channel_id=1, replica_groups=mesh['wide'=16,'narrow'=8] {'wide','narrow'}, dimensions={0} | all-to-all | bytes 131072 | tf_op jit(solution)/shard_map/all_to_all | solution.py:114
  110.3 0.1 copy.89
  110.4 11.7 %cholesky.18 = f32[128,128]{1,0:T(8,128)S(1)} custom-call(f32[128,128]{1,0:T(8,128)S(1)} %fusion.6), custom_call_target="Cholesky" | custom-call | tf_op jit(solution)/shard_map/jit(cholesky)/cholesky | solution.py:116
  122.2 0.6 compare_reduce_fusion
  122.8 0.7 select_bitcast_fusion
  123.5 0.7 copy.91
  (98 shorter events, 2.4 us)
Async XLA Ops:
  0.6 34.9 %copy-start = (f32[5,1,8,256]{3,2,1,0:T(8,128)S(1)}, f32[5,1,8,256]{3,2,1,0:T(8,128)}, u32[]{:S(2)}) copy-start(f32[5,1,8,256]{3,2,1,0:T(8,128)} %param.2) | copy-start | bytes 122884
  1.5 7.6 %collective-permute-start.1 = (bf16[5,1,8,256]{3,2,0,1:T(8,128)(2,1)S(1)}, bf16[5,1,8,256]{3,2,0,1:T(8,128)(2,1)S(1)}, u32[]{:S(2)}, u32[]{:S(2)}) collective-permute-start(bf16[5,1,8,256]{3,2,0,1:T(8,128)(2,1)S(1)} %bitcast_convert_fusion), channel_id=1, source_target_pairs={{8,0},{16,8},{24,16},{32,24},{40,32},{48,40},{56,48},{64,56},{72,6... | collective-permute-start | bytes 61448 | tf_op jit(solution)/shard_map/ppermute | solution.py:21
  2.9 6.2 %collective-permute-start = (bf16[5,1,8,256]{3,2,0,1:T(8,128)(2,1)S(1)}, bf16[5,1,8,256]{3,2,0,1:T(8,128)(2,1)S(1)}, u32[]{:S(2)}, u32[]{:S(2)}) collective-permute-start(bf16[5,1,8,256]{3,2,0,1:T(8,128)(2,1)S(1)} %bitcast_convert_fusion), channel_id=1, source_target_pairs={{0,8},{8,16},{16,24},{24,32},{32,40},{40,48},{48,56},{56,64},{64,7... | collective-permute-start | bytes 61448 | tf_op jit(solution)/shard_map/ppermute | solution.py:18
  9.1 6.0 %collective-permute-start.3 = (bf16[5,3,1,256]{3,2,0,1:T(2,128)(2,1)S(1)}, bf16[5,3,1,256]{3,2,0,1:T(2,128)(2,1)S(1)}, u32[]{:S(2)}, u32[]{:S(2)}) collective-permute-start(bf16[5,3,1,256]{3,2,0,1:T(2,128)(2,1)S(1)} %get-tuple-element.85), channel_id=1, source_target_pairs={{1,0},{2,1},{3,2},{4,3},{5,4},{6,5},{7,6},{0,7},{9,8},{10,9},{11,1... | collective-permute-start | bytes 23048 | tf_op jit(solution)/shard_map/ppermute | solution.py:21
  14.3 6.2 %collective-permute-start.2 = (bf16[5,3,1,256]{3,2,0,1:T(2,128)(2,1)S(1)}, bf16[5,3,1,256]{3,2,0,1:T(2,128)(2,1)S(1)}, u32[]{:S(2)}, u32[]{:S(2)}) collective-permute-start(bf16[5,3,1,256]{3,2,0,1:T(2,128)(2,1)S(1)} %get-tuple-element.84), channel_id=1, source_target_pairs={{0,1},{1,2},{2,3},{3,4},{4,5},{5,6},{6,7},{7,0},{8,9},{9,10},{10,1... | collective-permute-start | bytes 23048 | tf_op jit(solution)/shard_map/ppermute | solution.py:18
  21.7 5.7 %collective-permute-start.5 = (bf16[5,1,8,256]{3,2,0,1:T(8,128)(2,1)S(1)}, bf16[5,1,8,256]{3,2,0,1:T(8,128)(2,1)S(1)}, u32[]{:S(2)}, u32[]{:S(2)}) collective-permute-start(bf16[5,1,8,256]{3,2,0,1:T(8,128)(2,1)S(1)} %get-tuple-element.59), channel_id=1, source_target_pairs={{8,0},{16,8},{24,16},{32,24},{40,32},{48,40},{56,48},{64,56},{72,6... | collective-permute-start | bytes 61448 | tf_op jit(solution)/shard_map/ppermute | solution.py:21
  26.6 1.8 %collective-permute-start.4 = (bf16[5,1,8,256]{3,2,0,1:T(8,128)(2,1)S(1)}, bf16[5,1,8,256]{3,2,0,1:T(8,128)(2,1)S(1)}, u32[]{:S(2)}, u32[]{:S(2)}) collective-permute-start(bf16[5,1,8,256]{3,2,0,1:T(8,128)(2,1)S(1)} %get-tuple-element.59), channel_id=1, source_target_pairs={{0,8},{8,16},{16,24},{24,32},{32,40},{40,48},{48,56},{56,64},{64,7... | collective-permute-start | bytes 61448 | tf_op jit(solution)/shard_map/ppermute | solution.py:18
  28.4 4.2 %collective-permute-start.7 = (bf16[5,3,1,256]{3,2,0,1:T(2,128)(2,1)S(1)}, bf16[5,3,1,256]{3,2,0,1:T(2,128)(2,1)S(1)}, u32[]{:S(2)}, u32[]{:S(2)}) collective-permute-start(bf16[5,3,1,256]{3,2,0,1:T(2,128)(2,1)S(1)} %get-tuple-element.83), channel_id=1, source_target_pairs={{1,0},{2,1},{3,2},{4,3},{5,4},{6,5},{7,6},{0,7},{9,8},{10,9},{11,1... | collective-permute-start | bytes 23048 | tf_op jit(solution)/shard_map/ppermute | solution.py:21
  29.1 6.2 %collective-permute-start.6 = (bf16[5,3,1,256]{3,2,0,1:T(2,128)(2,1)S(1)}, bf16[5,3,1,256]{3,2,0,1:T(2,128)(2,1)S(1)}, u32[]{:S(2)}, u32[]{:S(2)}) collective-permute-start(bf16[5,3,1,256]{3,2,0,1:T(2,128)(2,1)S(1)} %get-tuple-element.82), channel_id=1, source_target_pairs={{0,1},{1,2},{2,3},{3,4},{4,5},{5,6},{6,7},{7,0},{8,9},{9,10},{10,1... | collective-permute-start | bytes 23048 | tf_op jit(solution)/shard_map/ppermute | solution.py:18
  35.8 7.0 %collective-permute-start.9 = (bf16[5,1,8,256]{3,2,0,1:T(8,128)(2,1)S(1)}, bf16[5,1,8,256]{3,2,0,1:T(8,128)(2,1)S(1)}, u32[]{:S(2)}, u32[]{:S(2)}) collective-permute-start(bf16[5,1,8,256]{3,2,0,1:T(8,128)(2,1)S(1)} %fusion.75), channel_id=1, source_target_pairs={{8,0},{16,8},{24,16},{32,24},{40,32},{48,40},{56,48},{64,56},{72,6... | collective-permute-start | bytes 61448 | tf_op jit(solution)/shard_map/ppermute | solution.py:21
  41.9 1.2 collective-permute-start.8
  43.2 4.2 %collective-permute-start.11 = (bf16[5,3,1,256]{3,2,0,1:T(2,128)(2,1)S(1)}, bf16[5,3,1,256]{3,2,0,1:T(2,128)(2,1)S(1)}, u32[]{:S(2)}, u32[]{:S(2)}) collective-permute-start(bf16[5,3,1,256]{3,2,0,1:T(2,128)(2,1)S(1)} %get-tuple-element.81), channel_id=1, source_target_pairs={{1,0},{2,1},{3,2},{4,3},{5,4},{6,5},{7,6},{0,7},{9,8},{10,9},{11,1... | collective-permute-start | bytes 23048 | tf_op jit(solution)/shard_map/ppermute | solution.py:21
  43.2 6.3 %collective-permute-start.10 = (bf16[5,3,1,256]{3,2,0,1:T(2,128)(2,1)S(1)}, bf16[5,3,1,256]{3,2,0,1:T(2,128)(2,1)S(1)}, u32[]{:S(2)}, u32[]{:S(2)}) collective-permute-start(bf16[5,3,1,256]{3,2,0,1:T(2,128)(2,1)S(1)} %get-tuple-element.80), channel_id=1, source_target_pairs={{0,1},{1,2},{2,3},{3,4},{4,5},{5,6},{6,7},{7,0},{8,9},{9,10},{10,1... | collective-permute-start | bytes 23048 | tf_op jit(solution)/shard_map/ppermute | solution.py:18
  49.7 19.1 %copy-start.1 = (bf16[124,5,1,2048]{3,0,2,1:T(8,128)(2,1)S(1)}, bf16[124,5,1,2048]{3,0,2,1:T(8,128)(2,1)}, u32[]{:S(2)}) copy-start(bf16[124,5,1,2048]{3,0,2,1:T(8,128)(2,1)} %param.3) | copy-start | bytes 7618564
  49.9 6.3 %collective-permute-start.13 = (bf16[5,1,8,256]{3,2,0,1:T(8,128)(2,1)S(1)}, bf16[5,1,8,256]{3,2,0,1:T(8,128)(2,1)S(1)}, u32[]{:S(2)}, u32[]{:S(2)}) collective-permute-start(bf16[5,1,8,256]{3,2,0,1:T(8,128)(2,1)S(1)} %get-tuple-element.25), channel_id=1, source_target_pairs={{8,0},{16,8},{24,16},{32,24},{40,32},{48,40},{56,48},{64,56},{72,6... | collective-permute-start | bytes 61448 | tf_op jit(solution)/shard_map/ppermute | solution.py:21
  55.4 1.2 collective-permute-start.12
  56.6 4.2 %collective-permute-start.15 = (bf16[5,3,1,256]{3,2,0,1:T(2,128)(2,1)S(1)}, bf16[5,3,1,256]{3,2,0,1:T(2,128)(2,1)S(1)}, u32[]{:S(2)}, u32[]{:S(2)}) collective-permute-start(bf16[5,3,1,256]{3,2,0,1:T(2,128)(2,1)S(1)} %get-tuple-element.79), channel_id=1, source_target_pairs={{1,0},{2,1},{3,2},{4,3},{5,4},{6,5},{7,6},{0,7},{9,8},{10,9},{11,1... | collective-permute-start | bytes 23048 | tf_op jit(solution)/shard_map/ppermute | solution.py:21
  56.7 6.3 %collective-permute-start.14 = (bf16[5,3,1,256]{3,2,0,1:T(2,128)(2,1)S(1)}, bf16[5,3,1,256]{3,2,0,1:T(2,128)(2,1)S(1)}, u32[]{:S(2)}, u32[]{:S(2)}) collective-permute-start(bf16[5,3,1,256]{3,2,0,1:T(2,128)(2,1)S(1)} %get-tuple-element.78), channel_id=1, source_target_pairs={{0,1},{1,2},{2,3},{3,4},{4,5},{5,6},{6,7},{7,0},{8,9},{9,10},{10,1... | collective-permute-start | bytes 23048 | tf_op jit(solution)/shard_map/ppermute | solution.py:18
  65.5 9.9 %all-to-all-start = ((bf16[8,2,2560]{2,1,0:T(2,128)(2,1)}), bf16[8,2,2560]{2,1,0:T(2,128)(2,1)S(1)}, u32[]{:S(2)}, u32[]{:S(2)}) async-start(bf16[8,2,2560]{2,1,0:T(2,128)(2,1)} %reshape.677), calls=%async_computation | async-start | bytes 163840 | tf_op jit(solution)/shard_map/all_to_all | solution.py:93
